TPU v7x, 512 devices: a whole 4x8x8 slice. The times are simulated.
512 devices in a mesh: row: 8 (over z_lo, core), bulk: 64 (over z_hi, x, y).
Axes of the slice: x: 4, y: 8, z: 8 (z_hi: 2, z_lo: 4; z = z_hi * 4 + z_lo), core: 2. Of those that a mesh axis runs over, the one named last changes fastest.
Arguments:
- residual_in: float32 [2048, 65536], P('row', 'bulk'), may hold values from -6 to 6
- amplitudes: float32 [2048, 2048], P('row', 'bulk'), may hold values from -6 to 6
- integral_tiles: float32 [4096, 128, 128], P('bulk', 'row'), may hold values from -0.1875 to 0.1875
- tile_reader: int32 [4096, 1], P('bulk'), may hold values from 0 to 63; in each aligned block of 64 rows (0 to 63, 64 to 127, ...) at most 2 rows name the same one
- tile_k: int32 [4096], P('bulk'), may hold values from 0 to 15
- tile_column: int32 [4096], P('bulk'), may hold values from 0 to 7
Outputs:
- residual_out: float32 [2048, 65536], P('row', 'bulk')
Inputs may be any that keep to these rules, and one draw needn't show every extreme that they name: `tile_reader`: among the 64 tiles stored on one index of bulk (aligned blocks of 64 entries), at most 2 name the same reader; some block has exactly 2 for some reader.
All inputs are finite; a program needn't handle non-finite values.
Results may differ from a plain program's by a relative error of at most 0.0003.
Values sent between devices are 32-bit elements; how exact they have to be, the bound alone decides.
A program may use at most 64 MiB of HBM per device.

v0:
```python
import jax
import jax.numpy as jnp
import numpy as np
from jax import lax
from jax.sharding import Mesh, PartitionSpec as P

KT = 16
CT = 8
SLOT = 2


def bucket_slots(tile_reader, tile_k, tile_column, targets, slots):
    readers = tile_reader[:, 0]
    matches = (readers[:, None] == jnp.arange(targets, dtype=jnp.int32)[None, :]).astype(jnp.int32)
    ordinal = jnp.cumsum(matches, axis=0) - matches
    position = jnp.sum(ordinal * matches, axis=1)
    select = matches.T[:, None, :] * (
        position[None, None, :] == jnp.arange(slots, dtype=jnp.int32)[None, :, None]
    ).astype(jnp.int32)
    filled = jnp.sum(select, axis=2)
    local_index = jnp.sum(
        select * jnp.arange(readers.shape[0], dtype=jnp.int32)[None, None, :], axis=2
    )
    slot_tile = jnp.sum(select * tile_k[None, None, :], axis=2) + filled - 1
    slot_column = jnp.sum(select * tile_column[None, None, :], axis=2) + filled - 1
    return (filled, local_index, slot_tile, slot_column)


def local(residual_in, amplitudes, integral_tiles, tile_reader, tile_k, tile_column):
    targets = lax.axis_size("bulk")
    height, width = (integral_tiles.shape[1], integral_tiles.shape[2])
    filled, local_index, slot_tile, slot_column = bucket_slots(
        tile_reader, tile_k, tile_column, targets, SLOT
    )
    picked = jnp.take(integral_tiles, local_index.reshape(-1), axis=0)
    picked = jnp.where(filled.reshape(-1)[:, None, None] > 0, picked, 0.0)
    outgoing = picked.reshape(targets, SLOT, height, width)
    arrived, arrived_tile, arrived_column = (
        lax.all_to_all(outgoing, "bulk", split_axis=0, concat_axis=0, tiled=True),
        lax.all_to_all(slot_tile, "bulk", split_axis=0, concat_axis=0, tiled=True),
        lax.all_to_all(slot_column, "bulk", split_axis=0, concat_axis=0, tiled=True),
    )
    arrived = arrived.reshape(targets * SLOT, height * width)
    position = arrived_tile.reshape(-1) * CT + arrived_column.reshape(-1)
    table = (position[None, :] == jnp.arange(KT * CT, dtype=jnp.int32)[:, None]).astype(jnp.float32)
    placed = jnp.dot(table, arrived, precision=lax.Precision.HIGHEST)
    placed = (
        placed.reshape(KT, CT, height, width).transpose(0, 2, 1, 3).reshape(KT * height, CT * width)
    )
    gathered = lax.all_gather(placed, "zl", axis=0, tiled=False)
    gathered = lax.all_gather(gathered, "core", axis=1, tiled=False)
    dense = gathered.reshape(-1, CT * width)
    amps = lax.all_gather(amplitudes, "bulk", axis=1, tiled=True)
    rows = amps.shape[0]
    groups = gathered.shape[0] * gathered.shape[1]
    amps = amps.reshape(rows, KT, groups, height).transpose(0, 2, 1, 3).reshape(rows, -1)
    return residual_in + jnp.dot(amps, dense, precision=lax.Precision.HIGHEST)


def solution(mesh):
    row_size = mesh.shape["row"]
    devices = np.asarray(mesh.devices).reshape(row_size // 2, 2, mesh.shape["bulk"])
    inner = Mesh(devices, ("zl", "core", "bulk"))
    row = ("zl", "core")
    placed = (
        P(row, "bulk"),
        P(row, "bulk"),
        P("bulk", row, None),
        P("bulk", None),
        P("bulk"),
        P("bulk"),
    )
    return jax.shard_map(
        local, mesh=inner, in_specs=placed, out_specs=P(row, "bulk"), check_vma=False
    )
```

profile of v0, /device:TPU:1, one launch (start us, length us, event | category | flops | bytes accessed | tf_op | source)
XLA Modules:
  0.0 376.1 jit_solution(10225368570562144597)
XLA Ops:
  6.5 0.0 copy-start
  6.5 0.8 fusion.9
  7.3 0.1 reduce_window_sum.11
  7.4 0.8 select_reduce_fusion
  8.3 0.9 fusion.1
  9.2 0.7 copy.34
  9.9 19.6 %all-to-all-start = ((s32[64,1,2]{2,1,0:T(1,128)}), s32[64,1,2]{2,1,0:T(1,128)S(1)}, u32[]{:S(2)}, u32[]{:S(2)}) async-start(s32[64,1,2]{2,1,0:T(1,128)} %copy.34), calls=%async_computation | async-start | bytes 65536 | tf_op jit(solution)/shard_map/all_to_all | solution.py:40
  29.5 0.1 copy.38
  29.6 0.1 reshape.184
  29.8 0.7 copy.35
  30.5 0.1 copy.36
  30.6 0.1 copy.37
  30.7 0.0 copy-done
  30.7 0.8 gather_fusion
  31.5 11.1 %all-to-all-done = s32[64,1,2]{2,1,0:T(1,128)S(1)} async-done(((s32[64,1,2]{2,1,0:T(1,128)}), s32[64,1,2]{2,1,0:T(1,128)S(1)}, u32[]{:S(2)}, u32[]{:S(2)}) %all-to-all-start) | async-done | bytes 544 | tf_op jit(solution)/shard_map/all_to_all | solution.py:40
  42.6 4.5 %all-to-all-start.1 = ((s32[64,1,2]{2,1,0:T(1,128)}), s32[64,1,2]{2,1,0:T(1,128)S(1)}, u32[]{:S(2)}, u32[]{:S(2)}) async-start(s32[64,1,2]{2,1,0:T(1,128)} %copy.35), calls=%async_computation.1 | async-start | bytes 65536 | tf_op jit(solution)/shard_map/all_to_all | solution.py:41
  47.2 1.3 select_select_fusion
  48.5 11.9 %all-to-all-done.1 = s32[64,1,2]{2,1,0:T(1,128)S(1)} async-done(((s32[64,1,2]{2,1,0:T(1,128)}), s32[64,1,2]{2,1,0:T(1,128)S(1)}, u32[]{:S(2)}, u32[]{:S(2)}) %all-to-all-start.1) | async-done | bytes 544 | tf_op jit(solution)/shard_map/all_to_all | solution.py:41
  60.4 4.7 %all-to-all-start.2 = ((f32[64,2,16,128]{3,2,1,0:T(8,128)}), f32[64,2,16,128]{3,2,1,0:T(8,128)S(1)}, u32[]{:S(2)}, u32[]{:S(2)}) async-start(f32[64,2,16,128]{3,2,1,0:T(8,128)} %select_select_fusion), calls=%async_computation.2 | async-start | bytes 2097152 | tf_op jit(solution)/shard_map/all_to_all | solution.py:39
  65.0 0.0 all-gather.5.cloned.1.call-start
  65.1 0.1 add_reduce_fusion
  65.2 0.1 add.82
  65.4 28.7 %all-to-all-done.2 = f32[64,2,16,128]{3,2,1,0:T(8,128)S(1)} async-done(((f32[64,2,16,128]{3,2,1,0:T(8,128)}), f32[64,2,16,128]{3,2,1,0:T(8,128)S(1)}, u32[]{:S(2)}, u32[]{:S(2)}) %all-to-all-start.2) | async-done | bytes 1048608 | tf_op jit(solution)/shard_map/all_to_all | solution.py:39
  94.0 0.3 copy.46
  94.4 0.3 copy.39
  94.7 0.7 convolution_bitcast_fusion.1
  95.4 0.0 copy-start.1
  95.4 1.1 all_gather_reshape.3
  96.6 0.0 all-gather.5.cloned.1.call-update
  96.6 0.0 all-gather.7.cloned.1.call-start
  96.6 0.7 all-gather.7.cloned.1.call-update
  97.3 0.2 all-gather.9.cloned.1.call-start
  97.6 84.4 %all-gather.5.cloned.1.call-done = f32[4,256,1024]{2,1,0:T(8,128)} async-done(((f32[1,256,1024]{2,1,0:T(8,128)}), f32[4,256,1024]{2,1,0:T(8,128)}) %all-gather.5.cloned.1.call-update) | async-done | bytes 4194320 | tf_op jit(solution)/shard_map/all_gather | solution.py:50
  182.0 0.0 all-gather.9.cloned.1.call-update
  182.0 0.0 copy-done.1
  182.0 1.3 copy.41
  183.3 138.8 %all-gather.7.cloned.1.call-done = f32[256,2048]{0,1:T(8,128)} async-done(((f32[256,32]{0,1:T(8,128)}), f32[256,2048]{0,1:T(8,128)}) %all-gather.7.cloned.1.call-update) | async-done | bytes 2097168 | tf_op jit(solution)/shard_map/all_gather | solution.py:53
  322.1 1.8 copy.40
  324.0 26.6 %all-gather.9.cloned.1.call-done = f32[4,512,1024]{2,1,0:T(8,128)} async-done(((f32[4,256,1024]{2,1,0:T(8,128)}), f32[4,512,1024]{2,1,0:T(8,128)}) %all-gather.9.cloned.1.call-update) | async-done | bytes 8388624 | tf_op jit(solution)/shard_map/all_gather | solution.py:51
  350.6 16.5 %fusion = f32[256,1024]{0,1:T(8,128)} fusion(f32[256,1024]{0,1:T(8,128)} %copy.41, f32[2048,1024]{1,0:T(8,128)} %bitcast.40, f32[256,2048]{0,1:T(8,128)S(1)} %bitcast.41), kind=kOutput, calls=%fused_computation.3 | convolution fusion | flops 6442713088 | bytes 12582912 | tf_op jit(solution)/shard_map/dot_general | solution.py:57
  367.1 2.5 copy.42
  (6 shorter events, 0.0 us)
Async XLA Ops:
  6.5 24.2 %copy-start = (f32[64,16,128]{2,1,0:T(8,128)S(1)}, f32[64,16,128]{2,1,0:T(8,128)}, u32[]{:S(2)}) copy-start(f32[64,16,128]{2,1,0:T(8,128)} %param.8) | copy-start | bytes 1572868
  9.9 32.7 %all-to-all-start = ((s32[64,1,2]{2,1,0:T(1,128)}), s32[64,1,2]{2,1,0:T(1,128)S(1)}, u32[]{:S(2)}, u32[]{:S(2)}) async-start(s32[64,1,2]{2,1,0:T(1,128)} %copy.34), calls=%async_computation | async-start | bytes 65536 | tf_op jit(solution)/shard_map/all_to_all | solution.py:40
  42.6 17.8 %all-to-all-start.1 = ((s32[64,1,2]{2,1,0:T(1,128)}), s32[64,1,2]{2,1,0:T(1,128)S(1)}, u32[]{:S(2)}, u32[]{:S(2)}) async-start(s32[64,1,2]{2,1,0:T(1,128)} %copy.35), calls=%async_computation.1 | async-start | bytes 65536 | tf_op jit(solution)/shard_map/all_to_all | solution.py:41
  60.4 33.6 %all-to-all-start.2 = ((f32[64,2,16,128]{3,2,1,0:T(8,128)}), f32[64,2,16,128]{3,2,1,0:T(8,128)S(1)}, u32[]{:S(2)}, u32[]{:S(2)}) async-start(f32[64,2,16,128]{3,2,1,0:T(8,128)} %select_select_fusion), calls=%async_computation.2 | async-start | bytes 2097152 | tf_op jit(solution)/shard_map/all_to_all | solution.py:39
  65.0 116.9 %all-gather.5.cloned.1.call-start = ((), (), s32[]{:S(2)}) async-start(), calls=%async_computation.3 | async-start | bytes 5242880 | tf_op jit(solution)/shard_map/all_gather | solution.py:50
  95.4 86.6 %copy-start.1 = (f32[256,1024]{1,0:T(8,128)S(1)}, f32[256,1024]{1,0:T(8,128)}, u32[]{:S(2)}) copy-start(f32[256,1024]{1,0:T(8,128)} %param.6) | copy-start | bytes 3145732
  96.6 225.6 %all-gather.7.cloned.1.call-start = ((), (), s32[]{:S(2)}) async-start(), calls=%async_computation.4 | async-start | bytes 2129920 | tf_op jit(solution)/shard_map/all_gather | solution.py:53
  97.3 253.2 %all-gather.9.cloned.1.call-start = ((), (), s32[]{:S(2)}) async-start(), calls=%async_computation.5 | async-start | bytes 12582912 | tf_op jit(solution)/shard_map/all_gather | solution.py:51
Sparse Core Ops, SparseCore 0:
  96.7 85.2 all-gather.4
  186.5 135.6 all-gather.6
  324.2 26.2 all-gather.8
where the time goes:
time: 377 us; the launch traced here: 376 us
  waiting for transfers between devices  302 us (80%)
  starting transfers between devices  29.1 us (8%)
  matrix products  17.2 us (5%)
  between operations  13.3 us (4%)
  local copies, waits for them, and re-layouts  10.2 us (3%)
  other arithmetic  4.08 us (1%)
    all_gather x1, waiting for transfers between devices, local(): amps = lax.all_gather(amplitudes, 'bulk', axis=1, tiled=True)  139 us
    all_gather x1, waiting for transfers between devices, local(): gathered = lax.all_gather(placed, 'zl', axis=0, tiled=False)  84.4 us
    all_to_all x1, waiting for transfers between devices, local(): lax.all_to_all(outgoing, 'bulk', split_axis=0, concat_axis=0, tiled=True)  28.7 us
    all_gather x1, waiting for transfers between devices, local(): gathered = lax.all_gather(gathered, 'core', axis=1, tiled=False)  26.6 us
    all_to_all x1, starting transfers between devices, local(): lax.all_to_all(slot_tile, 'bulk', split_axis=0, concat_axis=0, tiled=True)  19.6 us
    dot_general x1, matrix products, local(): return residual_in + jnp.dot(amps, dense, precision=lax.Precision.HIGHEST)  16.5 us
    all_to_all x1, waiting for transfers between devices, local(): lax.all_to_all(slot_column, 'bulk', split_axis=0, concat_axis=0, tiled=True)  11.9 us
    all_to_all x1, waiting for transfers between devices, local(): lax.all_to_all(slot_tile, 'bulk', split_axis=0, concat_axis=0, tiled=True)  11.1 us
  transfers between devices with their start and end apart: 6, of which 6 were waited for; matrix products, arithmetic and copies ran while one was open for 2% of the time, Pallas kernels for 0%

commit v1 on v0

--- a/solution.py
+++ b/solution.py
@@ -50,7 +50,8 @@
     gathered = lax.all_gather(placed, "zl", axis=0, tiled=False)
     gathered = lax.all_gather(gathered, "core", axis=1, tiled=False)
     dense = gathered.reshape(-1, CT * width)
-    amps = lax.all_gather(amplitudes, "bulk", axis=1, tiled=True)
+    outgoing_2 = jnp.stack([amplitudes] * lax.axis_size("bulk"))
+    amps = jnp.concatenate(lax.all_to_all(outgoing_2, "bulk", 0, 0), axis=1)
     rows = amps.shape[0]
     groups = gathered.shape[0] * gathered.shape[1]
     amps = amps.reshape(rows, KT, groups, height).transpose(0, 2, 1, 3).reshape(rows, -1)

time: 377 us -> 283 us (0.75)
  waiting for transfers between devices: 302 us -> 188 us
  starting transfers between devices: 29.1 us -> 43.5 us
  local copies, waits for them, and re-layouts: 10.2 us -> 15.3 us
    all_gather x1 -> x0, waiting for transfers between devices: 139 us -> none  [local(): amps = lax.all_gather(amplitudes, 'bulk', axis=1, tiled=True)]
    all_to_all x0 -> x1, waiting for transfers between devices: none -> 50.7 us  [local(): amps = jnp.concatenate(lax.all_to_all(outgoing_2, 'bulk', 0, 0), axis=1)]
    all_gather x1, waiting for transfers between devices: 26.6 us -> 0.02 us  [local(): gathered = lax.all_gather(gathered, 'core', axis=1, tiled=False)]
    all_to_all x0 -> x1, starting transfers between devices: none -> 14.7 us  [local(): amps = jnp.concatenate(lax.all_to_all(outgoing_2, 'bulk', 0, 0), axis=1)]
  transfers between devices with their start and end apart: 6 -> 6, of which waited for: 6 -> 5; matrix products, arithmetic and copies ran while one was open for 2% -> 3% of each run, Pallas kernels for 0% -> 0%
where the time goes in v1:
time: 283 us; the launch traced here: 282 us
  waiting for transfers between devices  188 us (66%)
  starting transfers between devices  43.5 us (15%)
  matrix products  17.2 us (6%)
  local copies, waits for them, and re-layouts  15.3 us (5%)
  between operations  13.6 us (5%)
  other arithmetic  4.08 us (1%)
    all_gather x1, waiting for transfers between devices, local(): gathered = lax.all_gather(placed, 'zl', axis=0, tiled=False)  85.3 us
    all_to_all x1, waiting for transfers between devices, local(): amps = jnp.concatenate(lax.all_to_all(outgoing_2, 'bulk', 0, 0), axis=1)  50.7 us
    all_to_all x1, waiting for transfers between devices, local(): lax.all_to_all(outgoing, 'bulk', split_axis=0, concat_axis=0, tiled=True)  28.7 us
    all_to_all x1, starting transfers between devices, local(): lax.all_to_all(slot_tile, 'bulk', split_axis=0, concat_axis=0, tiled=True)  19.6 us
    dot_general x1, matrix products, local(): return residual_in + jnp.dot(amps, dense, precision=lax.Precision.HIGHEST)  16.5 us
    all_to_all x1, starting transfers between devices, local(): amps = jnp.concatenate(lax.all_to_all(outgoing_2, 'bulk', 0, 0), axis=1)  14.7 us
    all_to_all x1, waiting for transfers between devices, local(): lax.all_to_all(slot_column, 'bulk', split_axis=0, concat_axis=0, tiled=True)  11.9 us
    all_to_all x1, waiting for transfers between devices, local(): lax.all_to_all(slot_tile, 'bulk', split_axis=0, concat_axis=0, tiled=True)  11.1 us
  transfers between devices with their start and end apart: 6, of which 5 were waited for; matrix products, arithmetic and copies ran while one was open for 3% of the time, Pallas kernels for 0%

profile of v1, /device:TPU:1, one launch (start us, length us, event | category | flops | bytes accessed | tf_op | source)
XLA Modules:
  0.0 281.5 jit_solution(14336092096046881125)
XLA Ops:
  6.5 0.0 copy-start
  6.5 0.8 fusion.9
  7.3 0.1 reduce_window_sum.11
  7.4 0.8 select_reduce_fusion
  8.3 0.9 fusion.1
  9.2 0.7 copy.29
  9.9 19.6 %all-to-all-start = ((s32[64,1,2]{2,1,0:T(1,128)}), s32[64,1,2]{2,1,0:T(1,128)S(1)}, u32[]{:S(2)}, u32[]{:S(2)}) async-start(s32[64,1,2]{2,1,0:T(1,128)} %copy.29), calls=%async_computation | async-start | bytes 65536 | tf_op jit(solution)/shard_map/all_to_all | solution.py:40
  29.5 0.1 copy.33
  29.6 0.1 reshape.186
  29.8 0.7 copy.30
  30.5 0.1 copy.31
  30.6 0.1 copy.32
  30.7 0.0 copy-done
  30.7 0.8 gather_fusion
  31.5 11.1 %all-to-all-done = s32[64,1,2]{2,1,0:T(1,128)S(1)} async-done(((s32[64,1,2]{2,1,0:T(1,128)}), s32[64,1,2]{2,1,0:T(1,128)S(1)}, u32[]{:S(2)}, u32[]{:S(2)}) %all-to-all-start) | async-done | bytes 544 | tf_op jit(solution)/shard_map/all_to_all | solution.py:40
  42.6 4.5 %all-to-all-start.1 = ((s32[64,1,2]{2,1,0:T(1,128)}), s32[64,1,2]{2,1,0:T(1,128)S(1)}, u32[]{:S(2)}, u32[]{:S(2)}) async-start(s32[64,1,2]{2,1,0:T(1,128)} %copy.30), calls=%async_computation.1 | async-start | bytes 65536 | tf_op jit(solution)/shard_map/all_to_all | solution.py:41
  47.2 1.3 select_select_fusion
  48.5 11.9 %all-to-all-done.1 = s32[64,1,2]{2,1,0:T(1,128)S(1)} async-done(((s32[64,1,2]{2,1,0:T(1,128)}), s32[64,1,2]{2,1,0:T(1,128)S(1)}, u32[]{:S(2)}, u32[]{:S(2)}) %all-to-all-start.1) | async-done | bytes 544 | tf_op jit(solution)/shard_map/all_to_all | solution.py:41
  60.4 4.7 %all-to-all-start.2 = ((f32[64,2,16,128]{3,2,1,0:T(8,128)}), f32[64,2,16,128]{3,2,1,0:T(8,128)S(1)}, u32[]{:S(2)}, u32[]{:S(2)}) async-start(f32[64,2,16,128]{3,2,1,0:T(8,128)} %select_select_fusion), calls=%async_computation.2 | async-start | bytes 2097152 | tf_op jit(solution)/shard_map/all_to_all | solution.py:39
  65.0 0.0 all-gather.4.cloned.1.call-start
  65.1 0.1 add_reduce_fusion
  65.2 0.1 add.82
  65.4 28.7 %all-to-all-done.2 = f32[64,2,16,128]{3,2,1,0:T(8,128)S(1)} async-done(((f32[64,2,16,128]{3,2,1,0:T(8,128)}), f32[64,2,16,128]{3,2,1,0:T(8,128)S(1)}, u32[]{:S(2)}, u32[]{:S(2)}) %all-to-all-start.2) | async-done | bytes 1048608 | tf_op jit(solution)/shard_map/all_to_all | solution.py:39
  94.0 0.3 copy.41
  94.4 0.3 copy.34
  94.7 0.7 convolution_bitcast_fusion.1
  95.4 1.1 all_gather_reshape.3
  96.5 0.0 all-gather.4.cloned.1.call-update
  96.6 0.0 all-gather.6.cloned.1.call-start
  96.6 85.3 %all-gather.4.cloned.1.call-done = f32[4,256,1024]{2,1,0:T(8,128)} async-done(((f32[1,256,1024]{2,1,0:T(8,128)}), f32[4,256,1024]{2,1,0:T(8,128)}) %all-gather.4.cloned.1.call-update) | async-done | bytes 4194320 | tf_op jit(solution)/shard_map/all_gather | solution.py:50
  181.9 0.0 copy-start.2
  181.9 0.0 all-gather.6.cloned.1.call-update
  182.0 0.7 copy-done.2
  182.7 1.6 stack.2
  184.3 14.7 %all-to-all-start.3 = ((f32[64,256,32]{1,2,0:T(8,128)}), f32[64,256,32]{1,2,0:T(8,128)S(1)}, u32[]{:S(2)}, u32[]{:S(2)}) async-start(f32[64,256,32]{1,2,0:T(8,128)} %stack.2), calls=%async_computation.3 | async-start | bytes 4194304 | tf_op jit(solution)/shard_map/all_to_all | solution.py:54
  199.0 2.7 copy.36
  201.7 50.7 %all-to-all-done.3 = f32[64,256,32]{1,2,0:T(8,128)S(1)} async-done(((f32[64,256,32]{1,2,0:T(8,128)}), f32[64,256,32]{1,2,0:T(8,128)S(1)}, u32[]{:S(2)}, u32[]{:S(2)}) %all-to-all-start.3) | async-done | bytes 2097184 | tf_op jit(solution)/shard_map/all_to_all | solution.py:54
  252.5 0.0 copy-start.1
  252.5 1.3 copy-done.1
  253.8 1.8 copy.35
  255.6 0.0 all-gather.6.cloned.1.call-done
  255.7 16.5 %fusion = f32[256,1024]{0,1:T(8,128)} fusion(f32[256,1024]{0,1:T(8,128)} %copy.36, f32[2048,1024]{1,0:T(8,128)} %bitcast.42, f32[256,2048]{0,1:T(8,128)S(1)} %bitcast.43), kind=kOutput, calls=%fused_computation.3 | convolution fusion | flops 6442713088 | bytes 12582912 | tf_op jit(solution)/shard_map/dot_general | solution.py:58
  272.2 2.5 copy.37
  (6 shorter events, 0.0 us)
Async XLA Ops:
  6.5 24.2 %copy-start = (f32[64,16,128]{2,1,0:T(8,128)S(1)}, f32[64,16,128]{2,1,0:T(8,128)}, u32[]{:S(2)}) copy-start(f32[64,16,128]{2,1,0:T(8,128)} %param.8) | copy-start | bytes 1572868
  9.9 32.7 %all-to-all-start = ((s32[64,1,2]{2,1,0:T(1,128)}), s32[64,1,2]{2,1,0:T(1,128)S(1)}, u32[]{:S(2)}, u32[]{:S(2)}) async-start(s32[64,1,2]{2,1,0:T(1,128)} %copy.29), calls=%async_computation | async-start | bytes 65536 | tf_op jit(solution)/shard_map/all_to_all | solution.py:40
  42.6 17.8 %all-to-all-start.1 = ((s32[64,1,2]{2,1,0:T(1,128)}), s32[64,1,2]{2,1,0:T(1,128)S(1)}, u32[]{:S(2)}, u32[]{:S(2)}) async-start(s32[64,1,2]{2,1,0:T(1,128)} %copy.30), calls=%async_computation.1 | async-start | bytes 65536 | tf_op jit(solution)/shard_map/all_to_all | solution.py:41
  60.4 33.6 %all-to-all-start.2 = ((f32[64,2,16,128]{3,2,1,0:T(8,128)}), f32[64,2,16,128]{3,2,1,0:T(8,128)S(1)}, u32[]{:S(2)}, u32[]{:S(2)}) async-start(f32[64,2,16,128]{3,2,1,0:T(8,128)} %select_select_fusion), calls=%async_computation.2 | async-start | bytes 2097152 | tf_op jit(solution)/shard_map/all_to_all | solution.py:39
  65.0 116.9 %all-gather.4.cloned.1.call-start = ((), (), s32[]{:S(2)}) async-start(), calls=%async_computation.4 | async-start | bytes 5242880 | tf_op jit(solution)/shard_map/all_gather | solution.py:50
  96.6 159.1 %all-gather.6.cloned.1.call-start = ((), (), s32[]{:S(2)}) async-start(), calls=%async_computation.5 | async-start | bytes 12582912 | tf_op jit(solution)/shard_map/all_gather | solution.py:51
  181.9 0.8 copy-start.2
  184.3 68.2 %all-to-all-start.3 = ((f32[64,256,32]{1,2,0:T(8,128)}), f32[64,256,32]{1,2,0:T(8,128)S(1)}, u32[]{:S(2)}, u32[]{:S(2)}) async-start(f32[64,256,32]{1,2,0:T(8,128)} %stack.2), calls=%async_computation.3 | async-start | bytes 4194304 | tf_op jit(solution)/shard_map/all_to_all | solution.py:54
  252.5 1.3 copy-start.1
Sparse Core Ops, SparseCore 0:
  96.7 85.2 all-gather.3
  184.0 29.6 all-gather.5
